TPU v7x, 32 devices: a whole 2x2x4 slice. The times are simulated.
32 devices in a mesh: tm: 8 (over z, core), dp: 2 (over y), rep: 2 (over x).
Axes of the slice: x: 2, y: 2, z: 4, core: 2. Of those that a mesh axis runs over, the one named last changes fastest.
Arguments:
- clip_frames: bfloat16 [4, 32, 8, 4, 256], P(('dp', 'rep'), 'tm'), may hold values from -6 to 6
- conv_weight: bfloat16 [3, 3, 3, 256, 256], replicated, may hold values from -0.078125 to 0.078125
- up_weight: bfloat16 [256, 1024], replicated, may hold values from -0.375 to 0.375
- cotangent: bfloat16 [4, 32, 8, 4, 1024], P(('dp', 'rep'), None, 'tm'), may hold values from -6 to 6
Outputs:
- input_grad: bfloat16 [4, 32, 8, 4, 256], P(('dp', 'rep'), 'tm')
- up_grad: float32 [256, 1024], P('tm', ('dp', 'rep'))
All inputs are finite; a program needn't handle non-finite values.
Results may differ from a plain program's by a relative error of at most 0.012.
Values may be sent and summed in bfloat16 or wider, within the bound.
No kernel may reach another device: no remote copies, remote signals or barrier semaphores. Data moves between devices by JAX's collectives and lax.ppermute only.
A program may use at most 128 MiB of HBM per device.

v0:
```python
import math

import jax
import jax.numpy as jnp
from jax import lax
from jax.sharding import PartitionSpec as P


def from_behind(value, axis, steps):
    count = lax.axis_size(axis)
    initial, last = (max(0, -steps), min(count, count - steps))
    return lax.ppermute(value, axis, [(source, source + steps) for source in range(initial, last)])


def correlate(source, kernel, frames):
    rows = source.shape[1] - 2
    cols = source.shape[2] - 2
    patches = []
    for shift_t in range(3):
        for shift_r in range(3):
            for shift_c in range(3):
                patches.append(
                    source[
                        shift_t : shift_t + frames,
                        shift_r : shift_r + rows,
                        shift_c : shift_c + cols,
                    ]
                )
    stacked = jnp.concatenate(patches, axis=-1)
    width = stacked.shape[-1]
    flat_kernel = kernel.reshape(width, kernel.shape[-1])
    return jnp.dot(stacked.reshape(-1, width), flat_kernel, preferred_element_type=jnp.float32)


def pad_space(field):
    return jnp.pad(field, ((0, 0), (1, 1), (1, 1), (0, 0)))


def local(clip_frames, conv_weight, up_weight, cotangent):
    frames_local = clip_frames[0]
    frames = frames_local.shape[0]
    rows = frames_local.shape[1]
    cols = frames_local.shape[2]
    chans = frames_local.shape[3]
    is_first = lax.axis_index("tm") == 0
    earlier = from_behind(frames_local[frames - 2 :], "tm", 1)
    earlier = jnp.where(is_first, jnp.broadcast_to(frames_local[:1], earlier.shape), earlier)
    source = pad_space(jnp.concatenate([earlier, frames_local], axis=0))
    pre = correlate(source, conv_weight, frames)
    hidden = jax.nn.silu(pre).astype(jnp.bfloat16).reshape(1, frames, rows, cols, chans)
    contract_rows = (((0,), (0,)), ((), ()))
    contract_cols = (((1,), (1,)), ((), ()))
    frame_cot = lax.all_to_all(cotangent, "tm", split_axis=1, concat_axis=2, tiled=True)
    flat_g = frame_cot.reshape(-1, frame_cot.shape[-1])
    term = lax.dot_general(
        hidden.reshape(-1, chans), flat_g, contract_rows, preferred_element_type=jnp.float32
    )
    hidden_grad = lax.dot_general(
        flat_g, up_weight, contract_cols, preferred_element_type=jnp.float32
    ).astype(jnp.bfloat16)
    sigma = jax.nn.sigmoid(pre)
    slope = sigma * (1.0 + pre * (1.0 - sigma))
    pre_grad = (hidden_grad.astype(jnp.float32) * slope).astype(jnp.bfloat16)
    pre_grad = pre_grad.reshape(frames, rows, cols, chans)
    later = from_behind(pre_grad[:2], "tm", -1)
    back_kernel = jnp.transpose(conv_weight[::-1, ::-1, ::-1], (0, 1, 2, 4, 3))
    grad_source = pad_space(jnp.concatenate([pre_grad, later], axis=0))
    input_grad = correlate(grad_source, back_kernel, frames).reshape(frames, rows, cols, chans)

    def edge_term():
        start = jnp.concatenate(
            [jnp.zeros((2, rows, cols, chans), jnp.bfloat16), pre_grad[:2]], axis=0
        )
        parts = correlate(pad_space(start), back_kernel, 2).reshape(2, rows, cols, chans)
        return parts[0] + parts[1]

    def no_term():
        return jnp.zeros((rows, cols, chans), jnp.float32)

    edge = lax.cond(is_first, edge_term, no_term)
    input_grad = input_grad.at[0].add(edge)
    time_count = lax.axis_size("tm")
    clip_count = lax.axis_size(("dp", "rep"))
    factor = 1.0 / math.sqrt(clip_count * frames * time_count * rows * cols)
    part = lax.psum_scatter(term, "tm", scatter_dimension=0, tiled=True)
    summed = lax.psum_scatter(part, ("dp", "rep"), scatter_dimension=1, tiled=True)
    return (input_grad.astype(jnp.bfloat16)[None], summed * factor)


def solution(mesh):
    in_specs = (
        P(("dp", "rep"), "tm", None, None, None),
        P(),
        P(),
        P(("dp", "rep"), None, "tm", None, None),
    )
    out_specs = (P(("dp", "rep"), "tm", None, None, None), P("tm", ("dp", "rep")))
    return jax.shard_map(local, mesh=mesh, in_specs=in_specs, out_specs=out_specs, check_vma=False)
```

profile of v0, /device:TPU:0, one launch (start us, length us, event | category | flops | bytes accessed | tf_op | source)
XLA Modules:
  0.0 133.0 jit_solution(5692337568943609760)
XLA Ops:
  7.2 0.8 slice_bitcast_fusion
  8.0 2.4 %collective-permute-start = (bf16[2,8,4,256]{3,2,1,0:T(4,128)(2,1)S(1)}, bf16[2,8,4,256]{3,2,1,0:T(4,128)(2,1)S(1)}, u32[]{:S(2)}, u32[]{:S(2)}) collective-permute-start(bf16[2,8,4,256]{3,2,1,0:T(4,128)(2,1)S(1)} %slice_bitcast_fusion), channel_id=1, source_target_pairs={{0,4},{4,8},{8,12},{12,16},{16,20},{20,24},{24,28},{1,5},{5,9},{9,... | collective-permute-start | bytes 98312 | tf_op jit(solution)/shard_map/ppermute | solution.py:12
  10.4 6.2 %all-to-all-start = ((bf16[1,32,1,4,1024]{4,3,2,0,1:T(4,128)(2,1)}), bf16[1,32,1,4,1024]{4,3,2,0,1:T(4,128)(2,1)S(1)}, u32[]{:S(2)}, u32[]{:S(2)}) async-start(bf16[1,32,1,4,1024]{4,3,2,0,1:T(4,128)(2,1)} %bitcast.45), calls=%async_computation | async-start | bytes 524288 | tf_op jit(solution)/shard_map/all_to_all | solution.py:53
  16.6 0.7 slice_bitcast_fusion.1
  17.4 6.1 %copy.24 = bf16[3,3,3,256,256]{3,4,2,1,0:T(8,128)(2,1)} copy(bf16[3,3,3,256,256]{4,3,2,1,0:T(8,128)(2,1)} %param.9) | data formatting | bytes 7077888 | tf_op args[1]
  23.5 4.2 %reverse_bitcast_fusion = bf16[3,3,3,256,256]{4,3,2,1,0:T(8,128)(2,1)} fusion(bf16[3,3,3,256,256]{3,4,2,1,0:T(8,128)(2,1)} %copy.24), kind=kLoop, calls=%fused_computation.180 | loop fusion | bytes 7077888 | tf_op jit(solution)/shard_map/transpose | solution.py:66
  27.7 4.1 %rev.3 = bf16[3,3,3,256,256]{3,4,2,1,0:T(8,128)(2,1)} reverse(bf16[3,3,3,256,256]{3,4,2,1,0:T(8,128)(2,1)} %copy.24), dimensions={0,1,2} | reverse | bytes 7077888 | tf_op jit(solution)/shard_map/rev | solution.py:66
  31.8 0.1 pad_maximum_fusion
  31.9 1.3 pad_slice_fusion.48
  33.2 0.8 pad_slice_fusion.49
  34.1 0.6 concatenate.77
  34.8 1.5 %concatenate.78 = bf16[128,256]{1,0:T(8,128)(2,1)} reshape(bf16[4,8,4,256]{3,2,1,0:T(4,128)(2,1)} %get-tuple-element.33) | data formatting | bytes 131072 | tf_op jit(solution)/shard_map/concatenate | solution.py:29
  36.3 1.5 %concatenate.79 = bf16[128,256]{1,0:T(8,128)(2,1)} reshape(bf16[4,8,4,256]{3,2,1,0:T(4,128)(2,1)} %get-tuple-element.34) | data formatting | bytes 131072 | tf_op jit(solution)/shard_map/concatenate | solution.py:29
  37.8 0.6 concatenate.80
  38.4 1.5 %concatenate.81 = bf16[128,256]{1,0:T(8,128)(2,1)} reshape(bf16[4,8,4,256]{3,2,1,0:T(4,128)(2,1)} %get-tuple-element.35) | data formatting | bytes 131072 | tf_op jit(solution)/shard_map/concatenate | solution.py:29
  39.9 1.5 %concatenate.82 = bf16[128,256]{1,0:T(8,128)(2,1)} reshape(bf16[4,8,4,256]{3,2,1,0:T(4,128)(2,1)} %get-tuple-element.36) | data formatting | bytes 131072 | tf_op jit(solution)/shard_map/concatenate | solution.py:29
  41.4 1.5 %concatenate.83 = bf16[128,256]{1,0:T(8,128)(2,1)} reshape(bf16[4,8,4,256]{3,2,1,0:T(4,128)(2,1)} %get-tuple-element.37) | data formatting | bytes 131072 | tf_op jit(solution)/shard_map/concatenate | solution.py:29
  42.9 1.5 %concatenate.84 = bf16[128,256]{1,0:T(8,128)(2,1)} reshape(bf16[4,8,4,256]{3,2,1,0:T(4,128)(2,1)} %get-tuple-element.38) | data formatting | bytes 131072 | tf_op jit(solution)/shard_map/concatenate | solution.py:29
  44.4 1.5 %concatenate.85 = bf16[128,256]{1,0:T(8,128)(2,1)} reshape(bf16[4,8,4,256]{3,2,1,0:T(4,128)(2,1)} %get-tuple-element.39) | data formatting | bytes 131072 | tf_op jit(solution)/shard_map/concatenate | solution.py:29
  45.9 0.6 concatenate.86
  46.5 0.6 concatenate.87
  47.4 0.9 concatenate.99
  48.4 0.9 concatenate.102
  49.2 0.8 constant_dynamic-update-slice_fusion.52
  50.1 0.8 constant_dynamic-update-slice_fusion.51
  50.9 0.8 constant_dynamic-update-slice_fusion.50
  51.8 0.8 constant_dynamic-update-slice_fusion.49
  52.6 0.8 constant_dynamic-update-slice_fusion.48
  53.4 0.8 constant_dynamic-update-slice_fusion.47
  54.3 0.8 constant_dynamic-update-slice_fusion.46
  55.1 0.8 constant_dynamic-update-slice_fusion.45
  56.0 0.8 constant_dynamic-update-slice_fusion.44
  56.8 0.8 constant_dynamic-update-slice_fusion.43
  57.7 0.8 constant_dynamic-update-slice_fusion.42
  58.7 2.6 %fusion.10 = f32[128,256]{1,0:T(8,128)S(1)} fusion(bf16[128,6912]{1,0:T(8,128)(2,1)S(1)} %constant_dynamic-update-slice_fusion.27, bf16[6912,256]{1,0:T(8,128)(2,1)} %bitcast.37), kind=kOutput, calls=%fused_computation.182 | convolution fusion | flops 452984832 | bytes 5439488 | tf_op jit(solution)/shard_map/dot_general | solution.py:32
  61.4 0.1 copy.33
  61.6 0.3 fusion.2
  61.9 1.3 fusion.3
  63.3 1.3 collective-permute-start.1
  64.6 4.0 %conditional.1 = (f32[1,8,4,256]{3,1,2,0:T(8,128)S(1)}) conditional(s32[]{:T(128)} %convert_element_type.26, () %tuple.20, (bf16[4,8,4,256]{3,2,1,0:T(4,128)(2,1)S(1)}, bf16[3,3,3,256,256]{4,3,2,1,0:T(8,128)(2,1)}) %tuple.21), branch_computations={%region_0.1_spmd, %region_1.2_spmd} | conditional | flops 226500608 | bytes 9175050 | solution.py:80
  65.7 0.2 reshape.110
  65.9 2.7 %fusion.9 = f32[64,256]{1,0:T(8,128)S(1)} fusion(bf16[64,6912]{1,0:T(8,128)(2,1)S(1)} %reshape.110, bf16[6912,256]{1,0:T(8,128)(2,1)} %bitcast.36), kind=kOutput, calls=%fused_computation.181 | convolution fusion | flops 226492416 | bytes 4489216 | tf_op jit(solution)/shard_map/cond/branch_1_fun/dot_general | solution.py:32
  69.3 1.5 %copy-done.1 = bf16[3,3,3,256,256]{3,4,2,1,0:T(8,128)(2,1)S(1)} copy-done((bf16[3,3,3,256,256]{3,4,2,1,0:T(8,128)(2,1)S(1)}, bf16[3,3,3,256,256]{3,4,2,1,0:T(8,128)(2,1)}, u32[]{:S(2)}) %copy-start.1) | copy-done | bytes 3538968
  70.8 0.7 fusion.11
  71.5 28.2 %reduce-scatter.3.cloned.1.call-done = f32[32,1024]{1,0:T(8,128)} async-done(((f32[256,1024]{1,0:T(8,128)}), f32[32,1024]{1,0:T(8,128)}) %reduce-scatter.3.cloned.1.call-update) | async-done | bytes 131088 | tf_op jit(solution)/shard_map/reduce_scatter | solution.py:85
  99.8 0.7 copy.26
  100.4 24.3 %reduce-scatter.5.cloned.1.call-done = f32[32,256]{1,0:T(8,128)} async-done(((f32[32,1024]{1,0:T(8,128)}), f32[32,256]{1,0:T(8,128)}) %reduce-scatter.5.cloned.1.call-update) | async-done | bytes 32784 | tf_op jit(solution)/shard_map/reduce_scatter | solution.py:86
  124.8 1.4 %broadcast_multiply_fusion = f32[32,256]{1,0:T(8,128)} fusion(f32[32,256]{1,0:T(8,128)} %reduce-scatter.5.cloned.1.call-done), kind=kLoop, calls=%fused_computation.177 | loop fusion | flops 8192 | bytes 65536 | tf_op jit(solution)/shard_map/mul | solution.py:87
  (116 shorter events, 2.1 us)
Async XLA Ops:
  7.2 54.4 %copy-start = (bf16[256,1024]{1,0:T(8,128)(2,1)S(1)}, bf16[256,1024]{1,0:T(8,128)(2,1)}, u32[]{:S(2)}) copy-start(bf16[256,1024]{1,0:T(8,128)(2,1)} %param.10) | copy-start | bytes 1572868
  8.0 23.8 %collective-permute-start = (bf16[2,8,4,256]{3,2,1,0:T(4,128)(2,1)S(1)}, bf16[2,8,4,256]{3,2,1,0:T(4,128)(2,1)S(1)}, u32[]{:S(2)}, u32[]{:S(2)}) collective-permute-start(bf16[2,8,4,256]{3,2,1,0:T(4,128)(2,1)S(1)} %slice_bitcast_fusion), channel_id=1, source_target_pairs={{0,4},{4,8},{8,12},{12,16},{16,20},{20,24},{24,28},{1,5},{5,9},{9,... | collective-permute-start | bytes 98312 | tf_op jit(solution)/shard_map/ppermute | solution.py:12
  10.4 50.9 %all-to-all-start = ((bf16[1,32,1,4,1024]{4,3,2,0,1:T(4,128)(2,1)}), bf16[1,32,1,4,1024]{4,3,2,0,1:T(4,128)(2,1)S(1)}, u32[]{:S(2)}, u32[]{:S(2)}) async-start(bf16[1,32,1,4,1024]{4,3,2,0,1:T(4,128)(2,1)} %bitcast.45), calls=%async_computation | async-start | bytes 524288 | tf_op jit(solution)/shard_map/all_to_all | solution.py:53
  16.6 83.1 %reduce-scatter.3.cloned.1.call-start = ((), (), s32[]{:S(2)}) async-start(), calls=%async_computation.3 | async-start | bytes 1179648 | tf_op jit(solution)/shard_map/reduce_scatter | solution.py:85
  23.5 4.2 %copy-start.2 = (bf16[1,4,8,4,256]{4,3,2,1,0:T(4,128)(2,1)S(1)}, bf16[1,4,8,4,256]{4,3,2,1,0:T(4,128)(2,1)}, u32[]{:S(2)}) copy-start(bf16[1,4,8,4,256]{4,3,2,1,0:T(4,128)(2,1)} %param.8) | copy-start | bytes 196612
  34.8 13.6 %copy-start.3 = (bf16[4,8,4,256]{3,2,1,0:T(4,128)(2,1)S(1)}, bf16[4,8,4,256]{3,2,1,0:T(4,128)(2,1)}, u32[]{:S(2)}) copy-start(bf16[4,8,4,256]{3,2,1,0:T(4,128)(2,1)} %get-tuple-element.50) | copy-start | bytes 196612
  38.4 9.9 %copy-start.4 = (bf16[4,8,4,256]{3,2,1,0:T(4,128)(2,1)S(1)}, bf16[4,8,4,256]{3,2,1,0:T(4,128)(2,1)}, u32[]{:S(2)}) copy-start(bf16[4,8,4,256]{3,2,1,0:T(4,128)(2,1)} %get-tuple-element.53) | copy-start | bytes 196612
  63.3 5.4 %collective-permute-start.1 = (bf16[2,8,4,256]{3,1,2,0:T(8,128)(2,1)S(1)}, bf16[2,8,4,256]{3,1,2,0:T(8,128)(2,1)S(1)}, u32[]{:S(2)}, u32[]{:S(2)}) collective-permute-start(bf16[2,8,4,256]{3,1,2,0:T(8,128)(2,1)S(1)} %copy.21), channel_id=1, source_target_pairs={{4,0},{8,4},{12,8},{16,12},{20,16},{24,20},{28,24},{5,1},{9,5},{13... | collective-permute-start | bytes 98312 | tf_op jit(solution)/shard_map/ppermute | solution.py:12
  64.6 60.2 %reduce-scatter.5.cloned.1.call-start = ((), (), s32[]{:S(2)}) async-start(), calls=%async_computation.4 | async-start | bytes 163840 | tf_op jit(solution)/shard_map/reduce_scatter | solution.py:86
  68.8 2.0 %copy-start.1 = (bf16[3,3,3,256,256]{3,4,2,1,0:T(8,128)(2,1)S(1)}, bf16[3,3,3,256,256]{3,4,2,1,0:T(8,128)(2,1)}, u32[]{:S(2)}) copy-start(bf16[3,3,3,256,256]{3,4,2,1,0:T(8,128)(2,1)} %rev.3) | copy-start | bytes 10616836
Sparse Core Ops, SparseCore 0:
  64.7 34.9 reduce-scatter.2
  102.4 22.2 reduce-scatter.4
where the time goes:
time: 135 us; the launch traced here: 133 us
  waiting for transfers between devices  52.6 us (39%)
  local copies, waits for them, and re-layouts  46.5 us (34%)
  between operations  14.6 us (11%)
  starting transfers between devices  9.93 us (7%)
  matrix products  7.64 us (6%)
  other arithmetic  1.54 us (1%)
    reduce_scatter x1, waiting for transfers between devices, local(): part = lax.psum_scatter(term, 'tm', scatter_dimension=0, tiled=True)  28.2 us
    reduce_scatter x1, waiting for transfers between devices, local(): lax.psum_scatter(part, ('dp', 'rep'), scatter_dimension=1, tiled=True)  24.3 us
    unnamed x65, local copies, waits for them, and re-layouts  18.1 us
    concatenate x30, local copies, waits for them, and re-layouts, correlate(): stacked = jnp.concatenate(patches, axis=-1)  15.1 us
    all_to_all x1, starting transfers between devices, local(): lax.all_to_all(cotangent, 'tm', split_axis=1, concat_axis=2, tiled=True)  6.16 us
    dot_general x3, matrix products, correlate(): jnp.dot(stacked.reshape(-1, width), flat_kernel, preferred_element_type=j...  6.01 us
    transpose x1, local copies, waits for them, and re-layouts, local(): back_kernel = jnp.transpose(conv_weight[::-1, ::-1, ::-1], (0, 1, 2, 4, 3))  4.21 us
    rev x1, local copies, waits for them, and re-layouts, local(): back_kernel = jnp.transpose(conv_weight[::-1, ::-1, ::-1], (0, 1, 2, 4, 3))  4.13 us
  transfers between devices with their start and end apart: 5, of which 2 were waited for; matrix products, arithmetic and copies ran while one was open for 38% of the time, Pallas kernels for 0%

commit v1 on v0

v1 whole, which is shorter than its diff:
```python
import functools
import math

import jax
import jax.numpy as jnp
from jax import lax
from jax.experimental import pallas as pl
from jax.experimental.pallas import tpu as pltpu
from jax.sharding import PartitionSpec as P


F32 = jnp.float32
BF16 = jnp.bfloat16
IN_VMEM = pl.BlockSpec(memory_space=pltpu.VMEM)
IN_HBM = pl.BlockSpec(memory_space=pltpu.HBM)
NT = (((1,), (1,)), ((), ()))
TN = (((0,), (0,)), ((), ()))
DIRECT = 4
MIB = 1024 * 1024


def limit(mib):
    return pltpu.CompilerParams(vmem_limit_bytes=mib * MIB)


def struct(shape, dtype):
    return jax.ShapeDtypeStruct(shape, dtype)


def in_hbm(*values):
    return [pltpu.with_memory_space_constraint(value, pltpu.HBM) for value in values]


def up_to(value, step):
    return -(-value // step) * step


def swap(value, axis, mask):
    count = lax.axis_size(axis)
    return lax.ppermute(value, axis, [(source, source ^ mask) for source in range(count)])


def swaps(values, axis, step):
    arrived = []
    for k, value in enumerate(values, 1):
        arrived.append(swap(value, axis, step * k))
    return arrived


def here():
    return lax.axis_index("tm")


def column_shift(block, cols, shift):
    if shift:
        col = lax.broadcasted_iota(jnp.int32, block.shape, 1) % cols
        inside = (col + shift >= 0) & (col + shift < cols)
        block = jnp.where(inside, block, 0.0)
    return block.astype(BF16)


def row_shift(flat, span, shift):
    edge = jnp.zeros((span, flat.shape[1]), flat.dtype)
    if shift < 0:
        return jnp.concatenate([edge, flat[:-span]], axis=0)
    if shift > 0:
        return jnp.concatenate([flat[span:], edge], axis=0)
    return flat


def pack_kernel(near, frames_hbm, *refs):
    parts, (frames_vmem, wide, sem) = refs[:-3], refs[-3:]
    copy = pltpu.make_async_copy(frames_hbm, frames_vmem, sem)
    copy.start()
    frames, rows, cols, chans = frames_vmem.shape
    edge = jnp.zeros((frames * cols, chans), F32)
    wide[0] = edge
    wide[rows + 1] = edge
    copy.wait()
    for r in range(rows):
        for t in range(frames):
            wide[r + 1, t * cols : (t + 1) * cols, :] = frames_vmem[t, r].astype(F32)
    me = here() // 2
    for k, part in enumerate(parts):
        part[...] = wide[pl.ds((me ^ k) * near, near + 2)].astype(BF16)


def pack(frames, near, chips):
    count, rows, cols, chans = frames.shape
    return pl.pallas_call(
        functools.partial(pack_kernel, near),
        out_shape=(struct((near + 2, count * cols, chans), BF16),) * chips,
        in_specs=[IN_HBM],
        out_specs=(IN_VMEM,) * chips,
        scratch_shapes=[
            pltpu.VMEM(frames.shape, BF16),
            pltpu.VMEM((rows + 2, count * cols, chans), F32),
            pltpu.SemaphoreType.DMA(()),
        ],
        name="pack",
        compiler_params=limit(8),
        cost_estimate=pl.CostEstimate(flops=20_000_000_000, transcendentals=0, bytes_accessed=2 * frames.size),
    )(*in_hbm(frames))


def project_kernel(cot_hbm, up_hbm, mate, g, hidden_grad, cot, up, wide, sems):
    copies = [
        pltpu.make_async_copy(cot_hbm, cot, sems.at[0]),
        pltpu.make_async_copy(up_hbm, up, sems.at[1]),
    ]
    for copy in copies:
        copy.start()
    slots, frames, own, cols, _ = cot.shape
    mine = here() % 2
    for source, core in ((mate, 1 - mine), (cot, mine)):
        if source is cot:
            copies[0].wait()
        for s in range(slots):
            for t in range(frames):
                for q in range(own):
                    base = (s * frames + t) * cols
                    wide[core, q, base : base + cols, :] = source[s, t, q].astype(F32)
    value = wide[...].reshape(g.shape).astype(BF16)
    g[...] = value
    copies[1].wait()
    hidden_grad[...] = lax.dot_general(value, up[...], NT, preferred_element_type=F32).astype(BF16)


def project(cot, up, mate):
    slots, count, own, cols, width = cot.shape
    places = 2 * slots * count * own * cols
    return pl.pallas_call(
        project_kernel,
        out_shape=(struct((places, width), BF16), struct((places, up.shape[0]), BF16)),
        in_specs=[IN_HBM, IN_HBM, IN_VMEM],
        out_specs=(IN_VMEM,) * 2,
        scratch_shapes=[
            pltpu.VMEM(cot.shape, BF16),
            pltpu.VMEM(up.shape, BF16),
            pltpu.VMEM((2, own, slots * count * cols, width), F32),
            pltpu.SemaphoreType.DMA((2,)),
        ],
        name="project",
        compiler_params=limit(16),
    )(*in_hbm(cot, up), mate)


def gather_kernel(*refs):
    parts, out = refs[:-1], refs[-1]
    me = here() // 2
    for k, part in enumerate(parts):
        out[me ^ k] = part[...]


def gather(parts):
    return pl.pallas_call(
        gather_kernel,
        out_shape=struct((len(parts),) + parts[0].shape, BF16),
        in_specs=[IN_VMEM] * len(parts),
        out_specs=IN_VMEM,
        name="gather",
        compiler_params=limit(4),
    )(*parts)


def by_parity(chans, size):
    row = lax.broadcasted_iota(jnp.int32, (chans, chans), 0)
    col = lax.broadcasted_iota(jnp.int32, (chans, chans), 1)
    block = row // size
    target = (block % 2) * (chans // 2) + (block // 2) * size + row % size
    return jnp.where(target == col, 1.0, 0.0).astype(BF16)


def rows_kernel(size, cols, direct, half_ref, other, weight, g, hidden_grad, *refs):
    chips, tall, block, chans = half_ref.shape
    near = tall - 2
    *outs, field, hidden, grads, term = refs
    backs, outs = outs[:chips], outs[chips:]
    length = 2 * chips * block
    base = up_to(2 * cols + 1, 8)
    me = here() // 2
    mine = here() % 2
    for source, core in ((half_ref, mine), (other, 1 - mine)):
        for z in range(chips):
            start = pl.multiple_of(base + (2 * z + core) * block, 8)
            for i in range(tall):
                field[i, pl.ds(start, block), :] = source[z, i].astype(F32)
    for t in range(1, 3):
        field[:, base - t * cols : base - (t - 1) * cols, :] = field[:, base : base + cols, :]
    total = jnp.zeros((near * length, chans), F32)
    for a in range(3):
        flats = []
        for c in range(3):
            start = base + (a - 2) * cols + c - 1
            flats.append(column_shift(field[:, start : start + length, :], cols, c - 1))
        left = jnp.concatenate(
            [
                flats[c][b : b + near].reshape(near * length, chans)
                for b in range(3)
                for c in range(3)
            ],
            axis=1,
        )
        right = weight[9 * a : 9 * a + 9].reshape(9 * chans, chans)
        total += jnp.dot(left, right, preferred_element_type=F32)
    sigma = 1.0 / (1.0 + jnp.exp(-total))
    ordered = jnp.dot(
        (total * sigma).astype(BF16), by_parity(chans, size), preferred_element_type=F32
    ).astype(BF16)
    half = chans // 2
    for p in range(2):
        hidden[p] = ordered[:, p * half : (p + 1) * half]
    product = lax.dot_general(hidden[mine], g[...], TN, preferred_element_type=F32)
    parts, _, lanes = term.shape
    for n in range(parts):
        term[n] = product[:, n * lanes : (n + 1) * lanes]
    if direct:
        spot = lax.axis_index(("dp", "rep"))
        outs[0][...] = term[spot]
        for k in range(1, parts):
            outs[k][...] = term[spot ^ k].astype(BF16)
    else:
        outs[0][...] = term[...]
    slope = sigma * (1.0 + total * (1.0 - sigma))
    value = (hidden_grad[...].astype(F32) * slope).astype(BF16).astype(F32)
    grads[:, :length, :] = value.reshape(near, length, chans)
    grads[:, length:, :] = jnp.zeros((near, grads.shape[1] - length, chans), F32)
    for k, back in enumerate(backs):
        start = pl.multiple_of((2 * (me ^ k) + mine) * block, 8)
        back[...] = grads[:, pl.ds(start, back.shape[1]), :].astype(BF16)


def rows_of(half_ref, other, weight, g, hidden_grad, size, cols, parts, direct):
    chips, tall, block, chans = half_ref.shape
    near = tall - 2
    length = 2 * chips * block
    lanes = g.shape[1] // parts
    half = chans // 2
    reach = block + 2 * cols
    if direct:
        outs = (struct((half, lanes), F32),) + (struct((half, lanes), BF16),) * (parts - 1)
    else:
        outs = (struct((parts, half, lanes), F32),)
    outs = (struct((near, reach, chans), BF16),) * chips + outs
    return pl.pallas_call(
        functools.partial(rows_kernel, size, cols, direct),
        out_shape=outs,
        in_specs=[IN_VMEM] * 5,
        out_specs=(IN_VMEM,) * len(outs),
        scratch_shapes=[
            pltpu.VMEM((tall, up_to(up_to(2 * cols + 1, 8) + length + 1, 8), chans), F32),
            pltpu.VMEM((2, near * length, half), BF16),
            pltpu.VMEM((near, up_to(length + 2 * cols, 8), chans), F32),
            pltpu.VMEM((parts, half, lanes), F32),
        ],
        name="rows",
        compiler_params=limit(32),
    )(half_ref, other, weight, g, hidden_grad)


def spread_kernel(size, received, mine, *refs):
    got, refs = refs[:received], refs[received:]
    chips = (len(refs) + 1) // 2
    backs, kept, sends = refs[: chips - 1], refs[chips - 1], refs[chips:]

    def total(block):
        rows = pl.ds(pl.multiple_of(block * size, size), size)
        value = mine[rows, :]
        for ref in got:
            value = value + ref[rows, :].astype(F32)
        return value

    me = here() // 2
    kept[...] = total(me)
    for k, (back, send) in enumerate(zip(backs, sends), 1):
        send[:size] = total(me ^ k).astype(BF16)
        near, reach, _ = back.shape
        for i in range(near):
            send[size + i * reach : size + (i + 1) * reach] = back[i]


def spread(mine, got, backs, size):
    half, width = mine.shape
    chips = half // size
    near, reach, _ = backs[0].shape
    send = struct((size + near * reach, width), BF16)
    return pl.pallas_call(
        functools.partial(spread_kernel, size, len(got)),
        out_shape=(struct((size, width), F32),) + (send,) * (chips - 1),
        in_specs=[IN_VMEM] * (1 + len(got) + len(backs)),
        out_specs=(IN_VMEM,) * chips,
        name="split_rows",
        compiler_params=limit(4),
    )(mine, *got, *backs)


def finish_kernel(size, factor, kept, weight, own, *refs):
    got, (summed, out, field) = refs[:-3], refs[-3:]
    frames, rows, cols, chans = out.shape
    near, reach, _ = own.shape
    me = here() // 2
    value = kept[...]
    for ref in got:
        value = value + ref[:size].astype(F32)
    summed[...] = value * factor
    for i in range(near):
        field[me * near + i, 8 : 8 + reach, :] = own[i].astype(F32)
        for k, ref in enumerate(got, 1):
            first = size + i * reach
            field[(me ^ k) * near + i, 8 : 8 + reach, :] = ref[first : first + reach].astype(F32)
    span = up_to(reach, 16)
    sums = [jnp.zeros((rows * span, chans), F32)] * 3
    for c in range(3):
        block = column_shift(field[:, 9 - c : 9 - c + span, :], cols, 1 - c)
        flat = block.reshape(rows * span, chans)
        for b in range(3):
            left = row_shift(flat, span, 1 - b)
            for a in range(3):
                sums[a] += lax.dot_general(
                    left, weight[9 * a + 3 * b + c], NT, preferred_element_type=F32
                )
    sums = [value.reshape(rows, span, chans) for value in sums]

    def at(a, t):
        return sums[a][:, t * cols : (t + 1) * cols]

    edge = jnp.where(here() == 0, at(0, 0) + at(0, 1) + at(1, 0), 0.0)
    for t in range(frames):
        value = at(0, t + 2) + at(1, t + 1) + at(2, t)
        if t == 0:
            value = value + edge
        out[t] = value.astype(BF16)


def finish(kept, weight, own, got, shape, size, factor):
    _, rows, _, chans = shape
    reach = own.shape[1]
    return pl.pallas_call(
        functools.partial(finish_kernel, size, factor),
        out_shape=(struct(kept.shape, F32), struct(shape, BF16)),
        in_specs=[IN_VMEM] * (3 + len(got)),
        out_specs=(IN_VMEM,) * 2,
        scratch_shapes=[pltpu.VMEM((rows, 16 + up_to(reach, 16), chans), F32)],
        name="finish",
        compiler_params=limit(16),
    )(kept, weight, own, *got)


def whole(clip_frames, conv_weight, up_weight, cotangent):
    frames_local = clip_frames[0]
    frames, rows, cols, chans = frames_local.shape
    width = up_weight.shape[1]
    time_count = lax.axis_size("tm")
    clip_count = lax.axis_size(("dp", "rep"))
    weight = conv_weight.reshape(27, chans, chans)
    factor = 1.0 / math.sqrt(clip_count * frames * time_count * rows * cols)
    size = chans // time_count
    chips = time_count // 2
    own_rows = rows // time_count
    direct = clip_count <= DIRECT and chips <= DIRECT and width == clip_count * chans

    cot = cotangent.reshape(time_count, frames, own_rows, cols, width)
    mate = swap(cot, "tm", 1)
    parts = pack(frames_local, 2 * own_rows, chips)
    arrived = swaps(parts[1:], "tm", 2)
    half = gather([parts[0]] + arrived)
    other = swap(half, "tm", 1)
    g, hidden_grad = project(cot, up_weight, mate)
    outs = rows_of(half, other, weight, g, hidden_grad, size, cols, clip_count, direct)
    (own, *backs), (mine, *sends) = outs[:chips], outs[chips:]
    if direct:
        arrived = swaps(sends, ("dp", "rep"), 1)
        kept, *sends = spread(mine, arrived, backs, size)
    else:
        value = lax.psum_scatter(mine, ("dp", "rep"), scatter_dimension=0, tiled=True)[0]
        pairs = [[s for s in range(time_count) if s % 2 == c] for c in range(2)]
        kept = lax.psum_scatter(
            value, "tm", scatter_dimension=0, axis_index_groups=pairs, tiled=True
        )
        empty = jnp.zeros((size, chans), BF16)
        sends = [jnp.concatenate([empty, back.reshape(-1, chans)], axis=0) for back in backs]
    arrived = swaps(sends, "tm", 2)
    if not direct:
        summed = kept * factor
        kept = jnp.zeros((size, chans), F32)
        input_grad = finish(kept, weight, own, arrived, frames_local.shape, size, factor)[1]
        return (input_grad[None], summed)
    summed, input_grad = finish(kept, weight, own, arrived, frames_local.shape, size, factor)
    return (input_grad[None], summed)


def solution(mesh):
    in_specs = (
        P(("dp", "rep"), "tm", None, None, None),
        P(),
        P(),
        P(("dp", "rep"), None, "tm", None, None),
    )
    out_specs = (P(("dp", "rep"), "tm", None, None, None), P("tm", ("dp", "rep")))
    return jax.shard_map(whole, mesh=mesh, in_specs=in_specs, out_specs=out_specs, check_vma=False)
```

time: 135 us -> 33.7 us (0.25); the launches traced: 133 us -> 33.5 us
  local copies, waits for them, and re-layouts: 46.5 us -> 0.01 us
  waiting for transfers between devices: 52.6 us -> 12.8 us
  between operations: 14.6 us -> 0.71 us
  matrix products: 7.64 us -> 0 us
  Pallas kernels: 0 us -> 6.13 us
  starting transfers between devices: 9.93 us -> 13.9 us
  other arithmetic: 1.54 us -> 0 us
    reduce_scatter x2 -> x0, waiting for transfers between devices: 52.6 us -> none  [the longest x1 28.2 us: local(): part = lax.psum_scatter(term, 'tm', scatter_dimension=0, tiled=True)]
    unnamed x65 -> x2, local copies, waits for them, and re-layouts: 18.1 us -> 0.01 us
    concatenate x32 -> x0, local copies, waits for them, and re-layouts: 15.1 us -> none  [the longest x30 15.1 us: correlate(): stacked = jnp.concatenate(patches, axis=-1)]
    ppermute x2 -> x11, waiting for transfers between devices: 0.01 us -> 12.8 us  [swap(): lax.ppermute(value, axis, [(source, source ^ mask) for source in range(co...]
    ppermute x2 -> x11, starting transfers between devices: 3.69 us -> 13.9 us  [swap(): lax.ppermute(value, axis, [(source, source ^ mask) for source in range(co...]
    dot_general x5 -> x0, matrix products: 7.64 us -> none  [the longest x3 6.01 us: correlate(): jnp.dot(stacked.reshape(-1, width), flat_kernel, preferred_element_type=j...]
    all_to_all x1 -> x0, starting transfers between devices: 6.16 us -> none  [local(): lax.all_to_all(cotangent, 'tm', split_axis=1, concat_axis=2, tiled=True)]
    pallas_call x0 -> x6, Pallas kernels: none -> 6.13 us  [the longest x1 1.79 us: rows_of(): pl.pallas_call(functools.partial(rows_kernel, size, cols, direct), out_sh...]
  transfers between devices with their start and end apart: 5 -> 11, of which waited for: 2 -> 8; matrix products, arithmetic and copies ran while one was open for 38% -> 0% of each run, Pallas kernels for 0% -> 8%
where the time goes in v1:
time: 33.7 us; the launch traced here: 33.5 us
  starting transfers between devices  13.9 us (41%)
  waiting for transfers between devices  12.8 us (38%)
  Pallas kernels  6.13 us (18%)
  between operations  0.71 us (2%)
    ppermute x11, starting transfers between devices, swap(): lax.ppermute(value, axis, [(source, source ^ mask) for source in range(co...  13.9 us
    ppermute x11, waiting for transfers between devices, swap(): lax.ppermute(value, axis, [(source, source ^ mask) for source in range(co...  12.8 us
    pallas_call x1, Pallas kernels, rows_of(): pl.pallas_call(functools.partial(rows_kernel, size, cols, direct), out_sh...  1.79 us
    pallas_call x1, Pallas kernels, finish(): pl.pallas_call(functools.partial(finish_kernel, size, factor), out_shape=...  1.76 us
    pallas_call x1, Pallas kernels, project(): pl.pallas_call(project_kernel, out_shape=(struct((places, width), BF16),...  1.49 us
    pallas_call x1, Pallas kernels, pack(): pl.pallas_call(functools.partial(pack_kernel, near), out_shape=(struct((n...  1.03 us
  transfers between devices with their start and end apart: 11, of which 8 were waited for; matrix products, arithmetic and copies ran while one was open for 0% of the time, Pallas kernels for 8%

profile of v1, /device:TPU:0, one launch (start us, length us, event | category | flops | bytes accessed | tf_op | source)
XLA Modules:
  0.0 33.5 jit_solution(1398826021252694199)
XLA Ops:
  0.6 0.6 %collective-permute-start.4 = (bf16[8,4,1,4,1024]{4,3,2,1,0:T(4,128)(2,1)}, bf16[8,4,1,4,1024]{4,3,2,1,0:T(4,128)(2,1)S(1)}, u32[]{:S(2)}, u32[]{:S(2)}) collective-permute-start(bf16[8,4,1,4,1024]{4,3,2,1,0:T(4,128)(2,1)} %bitcast.6), channel_id=1, source_target_pairs={{0,4},{4,0},{8,12},{12,8},{16,20},{20,16},{24,28},{28,24},{1,5},{5... | collective-permute-start | bytes 786440 | tf_op jit(solution)/shard_map/ppermute | solution.py:40
  1.2 0.0 copy-start
  1.2 1.0 %pack.1 = (bf16[4,16,256]{2,1,0:T(8,128)(2,1)S(1)}, bf16[4,16,256]{2,1,0:T(8,128)(2,1)S(1)}, bf16[4,16,256]{2,1,0:T(8,128)(2,1)S(1)}, bf16[4,16,256]{2,1,0:T(8,128)(2,1)S(1)}) custom-call(bf16[4,8,4,256]{3,2,1,0:T(4,128)(2,1)} %bitcast.8), custom_call_target="tpu_custom_call" | custom-call | flops 20000000000 | bytes 65536 | tf_op jit(solution)/shard_map/pack/pallas_call | solution.py:90
  2.2 2.6 %collective-permute-start = (bf16[4,16,256]{2,1,0:T(8,128)(2,1)S(1)}, bf16[4,16,256]{2,1,0:T(8,128)(2,1)S(1)}, u32[]{:S(2)}, u32[]{:S(2)}) collective-permute-start(bf16[4,16,256]{2,1,0:T(8,128)(2,1)S(1)} %get-tuple-element.23), channel_id=1, source_target_pairs={{0,8},{4,12},{8,0},{12,4},{16,24},{20,28},{24,16},{28,20},{1,9},{5... | collective-permute-start | bytes 98312 | tf_op jit(solution)/shard_map/ppermute | solution.py:40
  4.9 2.6 %collective-permute-start.1 = (bf16[4,16,256]{2,1,0:T(8,128)(2,1)S(1)}, bf16[4,16,256]{2,1,0:T(8,128)(2,1)S(1)}, u32[]{:S(2)}, u32[]{:S(2)}) collective-permute-start(bf16[4,16,256]{2,1,0:T(8,128)(2,1)S(1)} %get-tuple-element.24), channel_id=1, source_target_pairs={{0,16},{4,20},{8,24},{12,28},{16,0},{20,4},{24,8},{28,12},{1,17},{... | collective-permute-start | bytes 98312 | tf_op jit(solution)/shard_map/ppermute | solution.py:40
  7.5 0.0 collective-permute-start.2
  7.5 0.0 collective-permute-done.refs_1_
  7.5 2.7 %collective-permute-done.1.refs_2_ = bf16[4,16,256]{2,1,0:T(8,128)(2,1)S(1)} collective-permute-done((bf16[4,16,256]{2,1,0:T(8,128)(2,1)S(1)}, bf16[4,16,256]{2,1,0:T(8,128)(2,1)S(1)}, u32[]{:S(2)}, u32[]{:S(2)}) %collective-permute-start.1) | collective-permute-done | bytes 32800 | tf_op jit(solution)/shard_map/ppermute | solution.py:40
  10.2 3.0 %collective-permute-done.2.refs_3_ = bf16[4,16,256]{2,1,0:T(8,128)(2,1)S(1)} collective-permute-done((bf16[4,16,256]{2,1,0:T(8,128)(2,1)S(1)}, bf16[4,16,256]{2,1,0:T(8,128)(2,1)S(1)}, u32[]{:S(2)}, u32[]{:S(2)}) %collective-permute-start.2) | collective-permute-done | bytes 32800 | tf_op jit(solution)/shard_map/ppermute | solution.py:40
  13.2 0.1 collective-permute-start.3
  13.3 0.0 collective-permute-done.4.mate
  13.3 1.5 %project.1 = (bf16[256,1024]{1,0:T(8,128)(2,1)S(1)}, bf16[256,256]{1,0:T(8,128)(2,1)S(1)}) custom-call(bf16[8,4,1,4,1024]{4,3,2,1,0:T(4,128)(2,1)} %bitcast.7, bf16[256,1024]{1,0:T(8,128)(2,1)} %up_hbm.1, bf16[8,4,1,4,1024]{4,3,2,1,0:T(4,128)(2,1)S(1)} %collective-permute-done.4.mate), custom_call_target="tpu_custom_call" | custom-call | tf_op jit(solution)/shard_map/project/pallas_call | solution.py:132
  14.8 0.0 collective-permute-done.3.other
  14.8 0.0 copy-done
  14.8 1.8 %rows.1 = (bf16[2,24,256]{2,1,0:T(8,128)(2,1)S(1)}, bf16[2,24,256]{2,1,0:T(8,128)(2,1)S(1)}, bf16[2,24,256]{2,1,0:T(8,128)(2,1)S(1)}, bf16[2,24,256]{2,1,0:T(8,1...) custom-call(bf16[4,4,16,256]{3,2,1,0:T(8,128)(2,1)S(1)} %gather.1.ha, ...), custom_call_target="tpu_custom_call" | custom-call | tf_op jit(solution)/shard_map/rows/pallas_call | solution.py:245
  16.6 1.6 %collective-permute-start.5 = (bf16[128,256]{1,0:T(8,128)(2,1)S(1)}, bf16[128,256]{1,0:T(8,128)(2,1)S(1)}, u32[]{:S(2)}, u32[]{:S(2)}) collective-permute-start(bf16[128,256]{1,0:T(8,128)(2,1)S(1)} %get-tuple-element.29), channel_id=1, source_target_pairs={{0,1},{1,0},{2,3},{3,2},{4,5},{5,4},{6,7},{7,6},{8,9},{9,8},{10,11... | collective-permute-start | bytes 196616 | tf_op jit(solution)/shard_map/ppermute | solution.py:40
  18.2 1.5 %collective-permute-start.6 = (bf16[128,256]{1,0:T(8,128)(2,1)S(1)}, bf16[128,256]{1,0:T(8,128)(2,1)S(1)}, u32[]{:S(2)}, u32[]{:S(2)}) collective-permute-start(bf16[128,256]{1,0:T(8,128)(2,1)S(1)} %get-tuple-element.30), channel_id=1, source_target_pairs={{0,2},{1,3},{2,0},{3,1},{4,6},{5,7},{6,4},{7,5},{8,10},{9,11},{10,... | collective-permute-start | bytes 196616 | tf_op jit(solution)/shard_map/ppermute | solution.py:40
  19.7 0.5 %collective-permute-start.7 = (bf16[128,256]{1,0:T(8,128)(2,1)S(1)}, bf16[128,256]{1,0:T(8,128)(2,1)S(1)}, u32[]{:S(2)}, u32[]{:S(2)}) collective-permute-start(bf16[128,256]{1,0:T(8,128)(2,1)S(1)} %get-tuple-element.31), channel_id=1, source_target_pairs={{0,3},{1,2},{2,1},{3,0},{4,7},{5,6},{6,5},{7,4},{8,11},{9,10},{10,... | collective-permute-start | bytes 196616 | tf_op jit(solution)/shard_map/ppermute | solution.py:40
  20.2 1.0 %collective-permute-done.5.refs_0_ = bf16[128,256]{1,0:T(8,128)(2,1)S(1)} collective-permute-done((bf16[128,256]{1,0:T(8,128)(2,1)S(1)}, bf16[128,256]{1,0:T(8,128)(2,1)S(1)}, u32[]{:S(2)}, u32[]{:S(2)}) %collective-permute-start.5) | collective-permute-done | bytes 65568 | tf_op jit(solution)/shard_map/ppermute | solution.py:40
  21.2 1.3 %collective-permute-done.6.refs_1_ = bf16[128,256]{1,0:T(8,128)(2,1)S(1)} collective-permute-done((bf16[128,256]{1,0:T(8,128)(2,1)S(1)}, bf16[128,256]{1,0:T(8,128)(2,1)S(1)}, u32[]{:S(2)}, u32[]{:S(2)}) %collective-permute-start.6) | collective-permute-done | bytes 65568 | tf_op jit(solution)/shard_map/ppermute | solution.py:40
  22.4 2.4 %collective-permute-done.7.refs_2_ = bf16[128,256]{1,0:T(8,128)(2,1)S(1)} collective-permute-done((bf16[128,256]{1,0:T(8,128)(2,1)S(1)}, bf16[128,256]{1,0:T(8,128)(2,1)S(1)}, u32[]{:S(2)}, u32[]{:S(2)}) %collective-permute-start.7) | collective-permute-done | bytes 65568 | tf_op jit(solution)/shard_map/ppermute | solution.py:40
  24.9 0.1 collective-permute-start.8
  25.0 0.9 %collective-permute-start.9 = (bf16[80,256]{1,0:T(8,128)(2,1)S(1)}, bf16[80,256]{1,0:T(8,128)(2,1)S(1)}, u32[]{:S(2)}, u32[]{:S(2)}) collective-permute-start(bf16[80,256]{1,0:T(8,128)(2,1)S(1)} %get-tuple-element.38), channel_id=1, source_target_pairs={{0,16},{4,20},{8,24},{12,28},{16,0},{20,4},{24,8},{28,12},{1,17},{... | collective-permute-start | bytes 122888 | tf_op jit(solution)/shard_map/ppermute | solution.py:40
  25.9 3.4 %collective-permute-start.10 = (bf16[80,256]{1,0:T(8,128)(2,1)S(1)}, bf16[80,256]{1,0:T(8,128)(2,1)S(1)}, u32[]{:S(2)}, u32[]{:S(2)}) collective-permute-start(bf16[80,256]{1,0:T(8,128)(2,1)S(1)} %get-tuple-element.39), channel_id=1, source_target_pairs={{0,24},{4,28},{8,16},{12,20},{16,8},{20,12},{24,0},{28,4},{1,25},{... | collective-permute-start | bytes 122888 | tf_op jit(solution)/shard_map/ppermute | solution.py:40
  29.4 0.1 collective-permute-done.8.refs_0_
  29.4 0.5 %collective-permute-done.9.refs_1_ = bf16[80,256]{1,0:T(8,128)(2,1)S(1)} collective-permute-done((bf16[80,256]{1,0:T(8,128)(2,1)S(1)}, bf16[80,256]{1,0:T(8,128)(2,1)S(1)}, u32[]{:S(2)}, u32[]{:S(2)}) %collective-permute-start.9) | collective-permute-done | bytes 40992 | tf_op jit(solution)/shard_map/ppermute | solution.py:40
  30.0 1.8 %collective-permute-done.10.refs_2_ = bf16[80,256]{1,0:T(8,128)(2,1)S(1)} collective-permute-done((bf16[80,256]{1,0:T(8,128)(2,1)S(1)}, bf16[80,256]{1,0:T(8,128)(2,1)S(1)}, u32[]{:S(2)}, u32[]{:S(2)}) %collective-permute-start.10) | collective-permute-done | bytes 40992 | tf_op jit(solution)/shard_map/ppermute | solution.py:40
  31.8 1.8 %finish.1 = (f32[32,256]{1,0:T(8,128)}, bf16[4,8,4,256]{3,2,1,0:T(4,128)(2,1)}) custom-call(f32[32,256]{1,0:T(8,128)S(1)} %get-tuple-element.35.kept, bf16[27,256,256]{2,1,0:T(8,128)(2,1)S(1)} %bitcast.5, bf16[2,24,256]{2,1,0:T(8,128)(2,1)S(1)} %get-tuple-element.36.own, bf16[80,256]{1,0:T(8,128)(2,1)S(1)} %collective-permute-done.8.refs_0_, ...), custom_call_target="tpu_custom_call" | custom-call | tf_op jit(solution)/shard_map/finish/pallas_call | solution.py:338
  (2 shorter events, 0.1 us)
Async XLA Ops:
  0.6 12.7 %collective-permute-start.4 = (bf16[8,4,1,4,1024]{4,3,2,1,0:T(4,128)(2,1)}, bf16[8,4,1,4,1024]{4,3,2,1,0:T(4,128)(2,1)S(1)}, u32[]{:S(2)}, u32[]{:S(2)}) collective-permute-start(bf16[8,4,1,4,1024]{4,3,2,1,0:T(4,128)(2,1)} %bitcast.6), channel_id=1, source_target_pairs={{0,4},{4,0},{8,12},{12,8},{16,20},{20,16},{24,28},{28,24},{1,5},{5... | collective-permute-start | bytes 786440 | tf_op jit(solution)/shard_map/ppermute | solution.py:40
  1.2 13.6 %copy-start = (bf16[3,3,3,256,256]{4,3,2,1,0:T(8,128)(2,1)S(1)}, bf16[3,3,3,256,256]{4,3,2,1,0:T(8,128)(2,1)}, u32[]{:S(2)}) copy-start(bf16[3,3,3,256,256]{4,3,2,1,0:T(8,128)(2,1)} %param.5) | copy-start | bytes 10616836
  2.2 5.2 %collective-permute-start = (bf16[4,16,256]{2,1,0:T(8,128)(2,1)S(1)}, bf16[4,16,256]{2,1,0:T(8,128)(2,1)S(1)}, u32[]{:S(2)}, u32[]{:S(2)}) collective-permute-start(bf16[4,16,256]{2,1,0:T(8,128)(2,1)S(1)} %get-tuple-element.23), channel_id=1, source_target_pairs={{0,8},{4,12},{8,0},{12,4},{16,24},{20,28},{24,16},{28,20},{1,9},{5... | collective-permute-start | bytes 98312 | tf_op jit(solution)/shard_map/ppermute | solution.py:40
  4.9 5.3 %collective-permute-start.1 = (bf16[4,16,256]{2,1,0:T(8,128)(2,1)S(1)}, bf16[4,16,256]{2,1,0:T(8,128)(2,1)S(1)}, u32[]{:S(2)}, u32[]{:S(2)}) collective-permute-start(bf16[4,16,256]{2,1,0:T(8,128)(2,1)S(1)} %get-tuple-element.24), channel_id=1, source_target_pairs={{0,16},{4,20},{8,24},{12,28},{16,0},{20,4},{24,8},{28,12},{1,17},{... | collective-permute-start | bytes 98312 | tf_op jit(solution)/shard_map/ppermute | solution.py:40
  7.5 5.7 %collective-permute-start.2 = (bf16[4,16,256]{2,1,0:T(8,128)(2,1)S(1)}, bf16[4,16,256]{2,1,0:T(8,128)(2,1)S(1)}, u32[]{:S(2)}, u32[]{:S(2)}) collective-permute-start(bf16[4,16,256]{2,1,0:T(8,128)(2,1)S(1)} %get-tuple-element.25), channel_id=1, source_target_pairs={{0,24},{4,28},{8,16},{12,20},{16,8},{20,12},{24,0},{28,4},{1,25},{... | collective-permute-start | bytes 98312 | tf_op jit(solution)/shard_map/ppermute | solution.py:40
  13.2 1.6 %collective-permute-start.3 = (bf16[4,4,16,256]{3,2,1,0:T(8,128)(2,1)S(1)}, bf16[4,4,16,256]{3,2,1,0:T(8,128)(2,1)S(1)}, u32[]{:S(2)}, u32[]{:S(2)}) collective-permute-start(bf16[4,4,16,256]{3,2,1,0:T(8,128)(2,1)S(1)} %gather.1.half_ref), channel_id=1, source_target_pairs={{0,4},{4,0},{8,12},{12,8},{16,20},{20,16},{24,28},{28,24},{1,5},{5... | collective-permute-start | bytes 393224 | tf_op jit(solution)/shard_map/ppermute | solution.py:40
  16.6 4.6 %collective-permute-start.5 = (bf16[128,256]{1,0:T(8,128)(2,1)S(1)}, bf16[128,256]{1,0:T(8,128)(2,1)S(1)}, u32[]{:S(2)}, u32[]{:S(2)}) collective-permute-start(bf16[128,256]{1,0:T(8,128)(2,1)S(1)} %get-tuple-element.29), channel_id=1, source_target_pairs={{0,1},{1,0},{2,3},{3,2},{4,5},{5,4},{6,7},{7,6},{8,9},{9,8},{10,11... | collective-permute-start | bytes 196616 | tf_op jit(solution)/shard_map/ppermute | solution.py:40
  18.2 4.3 %collective-permute-start.6 = (bf16[128,256]{1,0:T(8,128)(2,1)S(1)}, bf16[128,256]{1,0:T(8,128)(2,1)S(1)}, u32[]{:S(2)}, u32[]{:S(2)}) collective-permute-start(bf16[128,256]{1,0:T(8,128)(2,1)S(1)} %get-tuple-element.30), channel_id=1, source_target_pairs={{0,2},{1,3},{2,0},{3,1},{4,6},{5,7},{6,4},{7,5},{8,10},{9,11},{10,... | collective-permute-start | bytes 196616 | tf_op jit(solution)/shard_map/ppermute | solution.py:40
  19.7 5.2 %collective-permute-start.7 = (bf16[128,256]{1,0:T(8,128)(2,1)S(1)}, bf16[128,256]{1,0:T(8,128)(2,1)S(1)}, u32[]{:S(2)}, u32[]{:S(2)}) collective-permute-start(bf16[128,256]{1,0:T(8,128)(2,1)S(1)} %get-tuple-element.31), channel_id=1, source_target_pairs={{0,3},{1,2},{2,1},{3,0},{4,7},{5,6},{6,5},{7,4},{8,11},{9,10},{10,... | collective-permute-start | bytes 196616 | tf_op jit(solution)/shard_map/ppermute | solution.py:40
  24.9 4.5 %collective-permute-start.8 = (bf16[80,256]{1,0:T(8,128)(2,1)S(1)}, bf16[80,256]{1,0:T(8,128)(2,1)S(1)}, u32[]{:S(2)}, u32[]{:S(2)}) collective-permute-start(bf16[80,256]{1,0:T(8,128)(2,1)S(1)} %get-tuple-element.37), channel_id=1, source_target_pairs={{0,8},{4,12},{8,0},{12,4},{16,24},{20,28},{24,16},{28,20},{1,9},{5... | collective-permute-start | bytes 122888 | tf_op jit(solution)/shard_map/ppermute | solution.py:40
  25.0 5.0 %collective-permute-start.9 = (bf16[80,256]{1,0:T(8,128)(2,1)S(1)}, bf16[80,256]{1,0:T(8,128)(2,1)S(1)}, u32[]{:S(2)}, u32[]{:S(2)}) collective-permute-start(bf16[80,256]{1,0:T(8,128)(2,1)S(1)} %get-tuple-element.38), channel_id=1, source_target_pairs={{0,16},{4,20},{8,24},{12,28},{16,0},{20,4},{24,8},{28,12},{1,17},{... | collective-permute-start | bytes 122888 | tf_op jit(solution)/shard_map/ppermute | solution.py:40
  25.9 5.8 %collective-permute-start.10 = (bf16[80,256]{1,0:T(8,128)(2,1)S(1)}, bf16[80,256]{1,0:T(8,128)(2,1)S(1)}, u32[]{:S(2)}, u32[]{:S(2)}) collective-permute-start(bf16[80,256]{1,0:T(8,128)(2,1)S(1)} %get-tuple-element.39), channel_id=1, source_target_pairs={{0,24},{4,28},{8,16},{12,20},{16,8},{20,12},{24,0},{28,4},{1,25},{... | collective-permute-start | bytes 122888 | tf_op jit(solution)/shard_map/ppermute | solution.py:40

commit v2 on v1

--- a/solution.py
+++ b/solution.py
@@ -259,9 +259,7 @@
 
 
 def spread_kernel(size, received, mine, *refs):
-    got, refs = refs[:received], refs[received:]
-    chips = (len(refs) + 1) // 2
-    backs, kept, sends = refs[: chips - 1], refs[chips - 1], refs[chips:]
+    got, kept, sends = refs[:received], refs[received], refs[received + 1 :]
 
     def total(block):
         rows = pl.ds(pl.multiple_of(block * size, size), size)
@@ -272,42 +270,50 @@
 
     me = here() // 2
     kept[...] = total(me)
-    for k, (back, send) in enumerate(zip(backs, sends), 1):
-        send[:size] = total(me ^ k).astype(BF16)
-        near, reach, _ = back.shape
-        for i in range(near):
-            send[size + i * reach : size + (i + 1) * reach] = back[i]
-
-
-def spread(mine, got, backs, size):
+    for k, send in enumerate(sends, 1):
+        send[...] = total(me ^ k).astype(BF16)
+
+
+def spread(mine, got, size):
     half, width = mine.shape
     chips = half // size
-    near, reach, _ = backs[0].shape
-    send = struct((size + near * reach, width), BF16)
     return pl.pallas_call(
         functools.partial(spread_kernel, size, len(got)),
-        out_shape=(struct((size, width), F32),) + (send,) * (chips - 1),
-        in_specs=[IN_VMEM] * (1 + len(got) + len(backs)),
+        out_shape=(struct((size, width), F32),) + (struct((size, width), BF16),) * (chips - 1),
+        in_specs=[IN_VMEM] * (1 + len(got)),
         out_specs=(IN_VMEM,) * chips,
         name="split_rows",
         compiler_params=limit(4),
-    )(mine, *got, *backs)
-
-
-def finish_kernel(size, factor, kept, weight, own, *refs):
-    got, (summed, out, field) = refs[:-3], refs[-3:]
+    )(mine, *got)
+
+
+def final_kernel(factor, mine, *refs):
+    value = mine[...]
+    for ref in refs[:-1]:
+        value = value + ref[...].astype(F32)
+    refs[-1][...] = value * factor
+
+
+def final(mine, got, factor):
+    return pl.pallas_call(
+        functools.partial(final_kernel, factor),
+        out_shape=struct(mine.shape, F32),
+        in_specs=[IN_VMEM] * (1 + len(got)),
+        out_specs=IN_VMEM,
+        name="final_sum",
+        compiler_params=limit(4),
+    )(mine, *got)
+
+
+def finish_kernel(weight, own, *refs):
+    got, (out, field) = refs[:-2], refs[-2:]
     frames, rows, cols, chans = out.shape
     near, reach, _ = own.shape
     me = here() // 2
-    value = kept[...]
-    for ref in got:
-        value = value + ref[:size].astype(F32)
-    summed[...] = value * factor
     for i in range(near):
         field[me * near + i, 8 : 8 + reach, :] = own[i].astype(F32)
         for k, ref in enumerate(got, 1):
-            first = size + i * reach
-            field[(me ^ k) * near + i, 8 : 8 + reach, :] = ref[first : first + reach].astype(F32)
+            field[(me ^ k) * near + i, 8 : 8 + reach, :] = ref[i].astype(F32)
     span = up_to(reach, 16)
     sums = [jnp.zeros((rows * span, chans), F32)] * 3
     for c in range(3):
@@ -332,18 +338,17 @@
         out[t] = value.astype(BF16)
 
 
-def finish(kept, weight, own, got, shape, size, factor):
+def finish(weight, own, got, shape):
     _, rows, _, chans = shape
-    reach = own.shape[1]
-    return pl.pallas_call(
-        functools.partial(finish_kernel, size, factor),
-        out_shape=(struct(kept.shape, F32), struct(shape, BF16)),
-        in_specs=[IN_VMEM] * (3 + len(got)),
-        out_specs=(IN_VMEM,) * 2,
-        scratch_shapes=[pltpu.VMEM((rows, 16 + up_to(reach, 16), chans), F32)],
+    return pl.pallas_call(
+        finish_kernel,
+        out_shape=struct(shape, BF16),
+        in_specs=[IN_VMEM] * (2 + len(got)),
+        out_specs=IN_VMEM,
+        scratch_shapes=[pltpu.VMEM((rows, 16 + up_to(own.shape[1], 16), chans), F32)],
         name="finish",
         compiler_params=limit(16),
-    )(kept, weight, own, *got)
+    )(weight, own, *got)
 
 
 def whole(clip_frames, conv_weight, up_weight, cotangent):
@@ -368,24 +373,20 @@
     g, hidden_grad = project(cot, up_weight, mate)
     outs = rows_of(half, other, weight, g, hidden_grad, size, cols, clip_count, direct)
     (own, *backs), (mine, *sends) = outs[:chips], outs[chips:]
+    returned = swaps(backs, "tm", 2)
     if direct:
         arrived = swaps(sends, ("dp", "rep"), 1)
-        kept, *sends = spread(mine, arrived, backs, size)
+        kept, *sends = spread(mine, arrived, size)
+        arrived = swaps(sends, "tm", 2)
+        summed = final(kept, arrived, factor)
     else:
         value = lax.psum_scatter(mine, ("dp", "rep"), scatter_dimension=0, tiled=True)[0]
         pairs = [[s for s in range(time_count) if s % 2 == c] for c in range(2)]
-        kept = lax.psum_scatter(
+        value = lax.psum_scatter(
             value, "tm", scatter_dimension=0, axis_index_groups=pairs, tiled=True
         )
-        empty = jnp.zeros((size, chans), BF16)
-        sends = [jnp.concatenate([empty, back.reshape(-1, chans)], axis=0) for back in backs]
-    arrived = swaps(sends, "tm", 2)
-    if not direct:
-        summed = kept * factor
-        kept = jnp.zeros((size, chans), F32)
-        input_grad = finish(kept, weight, own, arrived, frames_local.shape, size, factor)[1]
-        return (input_grad[None], summed)
-    summed, input_grad = finish(kept, weight, own, arrived, frames_local.shape, size, factor)
+        summed = value * factor
+    input_grad = finish(weight, own, returned, frames_local.shape)
     return (input_grad[None], summed)
 
 

time: 33.7 us -> 32.2 us (0.955)
  waiting for transfers between devices: 12.8 us -> 6.42 us
  starting transfers between devices: 13.9 us -> 18.2 us
  Pallas kernels: 6.13 us -> 6.74 us
    ppermute x11 -> x14, waiting for transfers between devices: 12.8 us -> 6.42 us  [swap(): lax.ppermute(value, axis, [(source, source ^ mask) for source in range(co...]
    ppermute x11 -> x14, starting transfers between devices: 13.9 us -> 18.2 us  [swap(): lax.ppermute(value, axis, [(source, source ^ mask) for source in range(co...]
    pallas_call x1 -> x2, Pallas kernels: 1.76 us -> 2.38 us  [the longest x1 1.75 us: finish(): pl.pallas_call(finish_kernel, out_shape=struct(shape, BF16), in_specs=[IN...]
  transfers between devices with their start and end apart: 11 -> 14, of which waited for: 8 -> 4; matrix products, arithmetic and copies ran while one was open for 0% -> 0% of each run, Pallas kernels for 8% -> 13%
where the time goes in v2:
time: 32.2 us; the launch traced here: 32.1 us
  starting transfers between devices  18.2 us (57%)
  Pallas kernels  6.74 us (21%)
  waiting for transfers between devices  6.42 us (20%)
  between operations  0.71 us (2%)
    ppermute x14, starting transfers between devices, swap(): lax.ppermute(value, axis, [(source, source ^ mask) for source in range(co...  18.2 us
    ppermute x14, waiting for transfers between devices, swap(): lax.ppermute(value, axis, [(source, source ^ mask) for source in range(co...  6.42 us
    pallas_call x1, Pallas kernels, rows_of(): pl.pallas_call(functools.partial(rows_kernel, size, cols, direct), out_sh...  1.79 us
    pallas_call x1, Pallas kernels, finish(): pl.pallas_call(finish_kernel, out_shape=struct(shape, BF16), in_specs=[IN...  1.75 us
    pallas_call x1, Pallas kernels, project(): pl.pallas_call(project_kernel, out_shape=(struct((places, width), BF16),...  1.49 us
    pallas_call x1, Pallas kernels, pack(): pl.pallas_call(functools.partial(pack_kernel, near), out_shape=(struct((n...  1.03 us
  transfers between devices with their start and end apart: 14, of which 4 were waited for; matrix products, arithmetic and copies ran while one was open for 0% of the time, Pallas kernels for 13%

profile of v2, /device:TPU:0, one launch (start us, length us, event | category | flops | bytes accessed | tf_op | source)
XLA Modules:
  0.0 32.1 jit_solution(2784486181978343307)
XLA Ops:
  0.6 0.6 %collective-permute-start.4 = (bf16[8,4,1,4,1024]{4,3,2,1,0:T(4,128)(2,1)}, bf16[8,4,1,4,1024]{4,3,2,1,0:T(4,128)(2,1)S(1)}, u32[]{:S(2)}, u32[]{:S(2)}) collective-permute-start(bf16[8,4,1,4,1024]{4,3,2,1,0:T(4,128)(2,1)} %bitcast.6), channel_id=1, source_target_pairs={{0,4},{4,0},{8,12},{12,8},{16,20},{20,16},{24,28},{28,24},{1,5},{5... | collective-permute-start | bytes 786440 | tf_op jit(solution)/shard_map/ppermute | solution.py:40
  1.2 0.0 copy-start
  1.2 1.0 %pack.1 = (bf16[4,16,256]{2,1,0:T(8,128)(2,1)S(1)}, bf16[4,16,256]{2,1,0:T(8,128)(2,1)S(1)}, bf16[4,16,256]{2,1,0:T(8,128)(2,1)S(1)}, bf16[4,16,256]{2,1,0:T(8,128)(2,1)S(1)}) custom-call(bf16[4,8,4,256]{3,2,1,0:T(4,128)(2,1)} %bitcast.9), custom_call_target="tpu_custom_call" | custom-call | flops 20000000000 | bytes 65536 | tf_op jit(solution)/shard_map/pack/pallas_call | solution.py:90
  2.2 2.6 %collective-permute-start = (bf16[4,16,256]{2,1,0:T(8,128)(2,1)S(1)}, bf16[4,16,256]{2,1,0:T(8,128)(2,1)S(1)}, u32[]{:S(2)}, u32[]{:S(2)}) collective-permute-start(bf16[4,16,256]{2,1,0:T(8,128)(2,1)S(1)} %get-tuple-element.21), channel_id=1, source_target_pairs={{0,8},{4,12},{8,0},{12,4},{16,24},{20,28},{24,16},{28,20},{1,9},{5... | collective-permute-start | bytes 98312 | tf_op jit(solution)/shard_map/ppermute | solution.py:40
  4.9 2.6 %collective-permute-start.1 = (bf16[4,16,256]{2,1,0:T(8,128)(2,1)S(1)}, bf16[4,16,256]{2,1,0:T(8,128)(2,1)S(1)}, u32[]{:S(2)}, u32[]{:S(2)}) collective-permute-start(bf16[4,16,256]{2,1,0:T(8,128)(2,1)S(1)} %get-tuple-element.22), channel_id=1, source_target_pairs={{0,16},{4,20},{8,24},{12,28},{16,0},{20,4},{24,8},{28,12},{1,17},{... | collective-permute-start | bytes 98312 | tf_op jit(solution)/shard_map/ppermute | solution.py:40
  7.5 0.0 collective-permute-start.2
  7.5 0.0 collective-permute-done.refs_1_
  7.5 2.7 %collective-permute-done.1.refs_2_ = bf16[4,16,256]{2,1,0:T(8,128)(2,1)S(1)} collective-permute-done((bf16[4,16,256]{2,1,0:T(8,128)(2,1)S(1)}, bf16[4,16,256]{2,1,0:T(8,128)(2,1)S(1)}, u32[]{:S(2)}, u32[]{:S(2)}) %collective-permute-start.1) | collective-permute-done | bytes 32800 | tf_op jit(solution)/shard_map/ppermute | solution.py:40
  10.2 3.0 %collective-permute-done.2.refs_3_ = bf16[4,16,256]{2,1,0:T(8,128)(2,1)S(1)} collective-permute-done((bf16[4,16,256]{2,1,0:T(8,128)(2,1)S(1)}, bf16[4,16,256]{2,1,0:T(8,128)(2,1)S(1)}, u32[]{:S(2)}, u32[]{:S(2)}) %collective-permute-start.2) | collective-permute-done | bytes 32800 | tf_op jit(solution)/shard_map/ppermute | solution.py:40
  13.2 0.1 collective-permute-start.3
  13.3 0.0 collective-permute-done.4.mate
  13.3 1.5 %project.1 = (bf16[256,1024]{1,0:T(8,128)(2,1)S(1)}, bf16[256,256]{1,0:T(8,128)(2,1)S(1)}) custom-call(bf16[8,4,1,4,1024]{4,3,2,1,0:T(4,128)(2,1)} %bitcast.7, bf16[256,1024]{1,0:T(8,128)(2,1)} %up_hbm.1, bf16[8,4,1,4,1024]{4,3,2,1,0:T(4,128)(2,1)S(1)} %collective-permute-done.4.mate), custom_call_target="tpu_custom_call" | custom-call | tf_op jit(solution)/shard_map/project/pallas_call | solution.py:132
  14.8 0.0 collective-permute-done.3.other
  14.8 0.0 copy-done
  14.8 1.8 %rows.1 = (bf16[2,24,256]{2,1,0:T(8,128)(2,1)S(1)}, bf16[2,24,256]{2,1,0:T(8,128)(2,1)S(1)}, bf16[2,24,256]{2,1,0:T(8,128)(2,1)S(1)}, bf16[2,24,256]{2,1,0:T(8,1...) custom-call(bf16[4,4,16,256]{3,2,1,0:T(8,128)(2,1)S(1)} %gather.1.ha, ...), custom_call_target="tpu_custom_call" | custom-call | tf_op jit(solution)/shard_map/rows/pallas_call | solution.py:245
  16.6 1.6 %collective-permute-start.8 = (bf16[128,256]{1,0:T(8,128)(2,1)S(1)}, bf16[128,256]{1,0:T(8,128)(2,1)S(1)}, u32[]{:S(2)}, u32[]{:S(2)}) collective-permute-start(bf16[128,256]{1,0:T(8,128)(2,1)S(1)} %get-tuple-element.31), channel_id=1, source_target_pairs={{0,1},{1,0},{2,3},{3,2},{4,5},{5,4},{6,7},{7,6},{8,9},{9,8},{10,11... | collective-permute-start | bytes 196616 | tf_op jit(solution)/shard_map/ppermute | solution.py:40
  18.2 1.5 %collective-permute-start.9 = (bf16[128,256]{1,0:T(8,128)(2,1)S(1)}, bf16[128,256]{1,0:T(8,128)(2,1)S(1)}, u32[]{:S(2)}, u32[]{:S(2)}) collective-permute-start(bf16[128,256]{1,0:T(8,128)(2,1)S(1)} %get-tuple-element.32), channel_id=1, source_target_pairs={{0,2},{1,3},{2,0},{3,1},{4,6},{5,7},{6,4},{7,5},{8,10},{9,11},{10,... | collective-permute-start | bytes 196616 | tf_op jit(solution)/shard_map/ppermute | solution.py:40
  19.7 0.5 %collective-permute-start.10 = (bf16[128,256]{1,0:T(8,128)(2,1)S(1)}, bf16[128,256]{1,0:T(8,128)(2,1)S(1)}, u32[]{:S(2)}, u32[]{:S(2)}) collective-permute-start(bf16[128,256]{1,0:T(8,128)(2,1)S(1)} %get-tuple-element.33), channel_id=1, source_target_pairs={{0,3},{1,2},{2,1},{3,0},{4,7},{5,6},{6,5},{7,4},{8,11},{9,10},{10,... | collective-permute-start | bytes 196616 | tf_op jit(solution)/shard_map/ppermute | solution.py:40
  20.2 0.0 collective-permute-start.5
  20.2 0.9 %collective-permute-start.6 = (bf16[2,24,256]{2,1,0:T(8,128)(2,1)S(1)}, bf16[2,24,256]{2,1,0:T(8,128)(2,1)S(1)}, u32[]{:S(2)}, u32[]{:S(2)}) collective-permute-start(bf16[2,24,256]{2,1,0:T(8,128)(2,1)S(1)} %get-tuple-element.28), channel_id=1, source_target_pairs={{0,16},{4,20},{8,24},{12,28},{16,0},{20,4},{24,8},{28,12},{1,17},{... | collective-permute-start | bytes 73736 | tf_op jit(solution)/shard_map/ppermute | solution.py:40
  21.1 0.0 collective-permute-done.8.refs_0_
  21.2 3.4 %collective-permute-start.7 = (bf16[2,24,256]{2,1,0:T(8,128)(2,1)S(1)}, bf16[2,24,256]{2,1,0:T(8,128)(2,1)S(1)}, u32[]{:S(2)}, u32[]{:S(2)}) collective-permute-start(bf16[2,24,256]{2,1,0:T(8,128)(2,1)S(1)} %get-tuple-element.29), channel_id=1, source_target_pairs={{0,24},{4,28},{8,16},{12,20},{16,8},{20,12},{24,0},{28,4},{1,25},{... | collective-permute-start | bytes 73736 | tf_op jit(solution)/shard_map/ppermute | solution.py:40
  24.6 0.0 collective-permute-done.9.refs_1_
  24.6 0.3 collective-permute-done.10.refs_2_
  24.9 0.1 collective-permute-start.11
  25.0 0.9 %collective-permute-start.12 = (bf16[32,256]{1,0:T(8,128)(2,1)S(1)}, bf16[32,256]{1,0:T(8,128)(2,1)S(1)}, u32[]{:S(2)}, u32[]{:S(2)}) collective-permute-start(bf16[32,256]{1,0:T(8,128)(2,1)S(1)} %get-tuple-element.36), channel_id=1, source_target_pairs={{0,16},{4,20},{8,24},{12,28},{16,0},{20,4},{24,8},{28,12},{1,17},{... | collective-permute-start | bytes 49160 | tf_op jit(solution)/shard_map/ppermute | solution.py:40
  25.9 0.0 collective-permute-done.5.refs_0_
  25.9 3.4 %collective-permute-start.13 = (bf16[32,256]{1,0:T(8,128)(2,1)S(1)}, bf16[32,256]{1,0:T(8,128)(2,1)S(1)}, u32[]{:S(2)}, u32[]{:S(2)}) collective-permute-start(bf16[32,256]{1,0:T(8,128)(2,1)S(1)} %get-tuple-element.37), channel_id=1, source_target_pairs={{0,24},{4,28},{8,16},{12,20},{16,8},{20,12},{24,0},{28,4},{1,25},{... | collective-permute-start | bytes 49160 | tf_op jit(solution)/shard_map/ppermute | solution.py:40
  29.4 0.0 collective-permute-done.6.refs_1_
  29.4 0.0 collective-permute-done.7.refs_2_
  29.4 1.8 %finish.1 = bf16[4,8,4,256]{3,2,1,0:T(4,128)(2,1)} custom-call(bf16[27,256,256]{2,1,0:T(8,128)(2,1)S(1)} %bitcast.5, bf16[2,24,256]{2,1,0:T(8,128)(2,1)S(1)} %get-tuple-element.26.own, bf16[2,24,256]{2,1,0:T(8,128)(2,1)S(1)} %collective-permute-done.5.refs_0_, bf16[2,24,256]{2,1,0:T(8,128)(2,1)S(1)} %collective-permute-done.6.refs_1_, ...), custom_call_target="tpu_custom_call" | custom-call | tf_op jit(solution)/shard_map/finish/pallas_call | solution.py:343
  31.1 0.0 collective-permute-done.11.refs_0_
  31.1 0.0 collective-permute-done.12.refs_1_
  31.1 0.3 %collective-permute-done.13.refs_2_ = bf16[32,256]{1,0:T(8,128)(2,1)S(1)} collective-permute-done((bf16[32,256]{1,0:T(8,128)(2,1)S(1)}, bf16[32,256]{1,0:T(8,128)(2,1)S(1)}, u32[]{:S(2)}, u32[]{:S(2)}) %collective-permute-start.13) | collective-permute-done | bytes 16416 | tf_op jit(solution)/shard_map/ppermute | solution.py:40
  31.5 0.6 %final_sum.1 = f32[32,256]{1,0:T(8,128)} custom-call(f32[32,256]{1,0:T(8,128)S(1)} %get-tuple-element.34.mine, bf16[32,256]{1,0:T(8,128)(2,1)S(1)} %collective-permute-done.11.refs_0_, bf16[32,256]{1,0:T(8,128)(2,1)S(1)} %collective-permute-done.12.refs_1_, bf16[32,256]{1,0:T(8,128)(2,1)S(1)} %collective-permute-done.13.refs_2_), custom_call_target="tpu_custom_call" | custom-call | tf_op jit(solution)/shard_map/final_sum/pallas_call | solution.py:298
  (2 shorter events, 0.0 us)
Async XLA Ops:
  0.6 12.7 %collective-permute-start.4 = (bf16[8,4,1,4,1024]{4,3,2,1,0:T(4,128)(2,1)}, bf16[8,4,1,4,1024]{4,3,2,1,0:T(4,128)(2,1)S(1)}, u32[]{:S(2)}, u32[]{:S(2)}) collective-permute-start(bf16[8,4,1,4,1024]{4,3,2,1,0:T(4,128)(2,1)} %bitcast.6), channel_id=1, source_target_pairs={{0,4},{4,0},{8,12},{12,8},{16,20},{20,16},{24,28},{28,24},{1,5},{5... | collective-permute-start | bytes 786440 | tf_op jit(solution)/shard_map/ppermute | solution.py:40
  1.2 13.6 %copy-start = (bf16[3,3,3,256,256]{4,3,2,1,0:T(8,128)(2,1)S(1)}, bf16[3,3,3,256,256]{4,3,2,1,0:T(8,128)(2,1)}, u32[]{:S(2)}) copy-start(bf16[3,3,3,256,256]{4,3,2,1,0:T(8,128)(2,1)} %param.5) | copy-start | bytes 10616836
  2.2 5.2 %collective-permute-start = (bf16[4,16,256]{2,1,0:T(8,128)(2,1)S(1)}, bf16[4,16,256]{2,1,0:T(8,128)(2,1)S(1)}, u32[]{:S(2)}, u32[]{:S(2)}) collective-permute-start(bf16[4,16,256]{2,1,0:T(8,128)(2,1)S(1)} %get-tuple-element.21), channel_id=1, source_target_pairs={{0,8},{4,12},{8,0},{12,4},{16,24},{20,28},{24,16},{28,20},{1,9},{5... | collective-permute-start | bytes 98312 | tf_op jit(solution)/shard_map/ppermute | solution.py:40
  4.9 5.3 %collective-permute-start.1 = (bf16[4,16,256]{2,1,0:T(8,128)(2,1)S(1)}, bf16[4,16,256]{2,1,0:T(8,128)(2,1)S(1)}, u32[]{:S(2)}, u32[]{:S(2)}) collective-permute-start(bf16[4,16,256]{2,1,0:T(8,128)(2,1)S(1)} %get-tuple-element.22), channel_id=1, source_target_pairs={{0,16},{4,20},{8,24},{12,28},{16,0},{20,4},{24,8},{28,12},{1,17},{... | collective-permute-start | bytes 98312 | tf_op jit(solution)/shard_map/ppermute | solution.py:40
  7.5 5.7 %collective-permute-start.2 = (bf16[4,16,256]{2,1,0:T(8,128)(2,1)S(1)}, bf16[4,16,256]{2,1,0:T(8,128)(2,1)S(1)}, u32[]{:S(2)}, u32[]{:S(2)}) collective-permute-start(bf16[4,16,256]{2,1,0:T(8,128)(2,1)S(1)} %get-tuple-element.23), channel_id=1, source_target_pairs={{0,24},{4,28},{8,16},{12,20},{16,8},{20,12},{24,0},{28,4},{1,25},{... | collective-permute-start | bytes 98312 | tf_op jit(solution)/shard_map/ppermute | solution.py:40
  13.2 1.6 %collective-permute-start.3 = (bf16[4,4,16,256]{3,2,1,0:T(8,128)(2,1)S(1)}, bf16[4,4,16,256]{3,2,1,0:T(8,128)(2,1)S(1)}, u32[]{:S(2)}, u32[]{:S(2)}) collective-permute-start(bf16[4,4,16,256]{3,2,1,0:T(8,128)(2,1)S(1)} %gather.1.half_ref), channel_id=1, source_target_pairs={{0,4},{4,0},{8,12},{12,8},{16,20},{20,16},{24,28},{28,24},{1,5},{5... | collective-permute-start | bytes 393224 | tf_op jit(solution)/shard_map/ppermute | solution.py:40
  16.6 4.6 %collective-permute-start.8 = (bf16[128,256]{1,0:T(8,128)(2,1)S(1)}, bf16[128,256]{1,0:T(8,128)(2,1)S(1)}, u32[]{:S(2)}, u32[]{:S(2)}) collective-permute-start(bf16[128,256]{1,0:T(8,128)(2,1)S(1)} %get-tuple-element.31), channel_id=1, source_target_pairs={{0,1},{1,0},{2,3},{3,2},{4,5},{5,4},{6,7},{7,6},{8,9},{9,8},{10,11... | collective-permute-start | bytes 196616 | tf_op jit(solution)/shard_map/ppermute | solution.py:40
  18.2 6.4 %collective-permute-start.9 = (bf16[128,256]{1,0:T(8,128)(2,1)S(1)}, bf16[128,256]{1,0:T(8,128)(2,1)S(1)}, u32[]{:S(2)}, u32[]{:S(2)}) collective-permute-start(bf16[128,256]{1,0:T(8,128)(2,1)S(1)} %get-tuple-element.32), channel_id=1, source_target_pairs={{0,2},{1,3},{2,0},{3,1},{4,6},{5,7},{6,4},{7,5},{8,10},{9,11},{10,... | collective-permute-start | bytes 196616 | tf_op jit(solution)/shard_map/ppermute | solution.py:40
  19.7 5.2 %collective-permute-start.10 = (bf16[128,256]{1,0:T(8,128)(2,1)S(1)}, bf16[128,256]{1,0:T(8,128)(2,1)S(1)}, u32[]{:S(2)}, u32[]{:S(2)}) collective-permute-start(bf16[128,256]{1,0:T(8,128)(2,1)S(1)} %get-tuple-element.33), channel_id=1, source_target_pairs={{0,3},{1,2},{2,1},{3,0},{4,7},{5,6},{6,5},{7,4},{8,11},{9,10},{10,... | collective-permute-start | bytes 196616 | tf_op jit(solution)/shard_map/ppermute | solution.py:40
  20.2 5.8 %collective-permute-start.5 = (bf16[2,24,256]{2,1,0:T(8,128)(2,1)S(1)}, bf16[2,24,256]{2,1,0:T(8,128)(2,1)S(1)}, u32[]{:S(2)}, u32[]{:S(2)}) collective-permute-start(bf16[2,24,256]{2,1,0:T(8,128)(2,1)S(1)} %get-tuple-element.27), channel_id=1, source_target_pairs={{0,8},{4,12},{8,0},{12,4},{16,24},{20,28},{24,16},{28,20},{1,9},{5... | collective-permute-start | bytes 73736 | tf_op jit(solution)/shard_map/ppermute | solution.py:40
  20.2 9.2 %collective-permute-start.6 = (bf16[2,24,256]{2,1,0:T(8,128)(2,1)S(1)}, bf16[2,24,256]{2,1,0:T(8,128)(2,1)S(1)}, u32[]{:S(2)}, u32[]{:S(2)}) collective-permute-start(bf16[2,24,256]{2,1,0:T(8,128)(2,1)S(1)} %get-tuple-element.28), channel_id=1, source_target_pairs={{0,16},{4,20},{8,24},{12,28},{16,0},{20,4},{24,8},{28,12},{1,17},{... | collective-permute-start | bytes 73736 | tf_op jit(solution)/shard_map/ppermute | solution.py:40
  21.2 8.2 %collective-permute-start.7 = (bf16[2,24,256]{2,1,0:T(8,128)(2,1)S(1)}, bf16[2,24,256]{2,1,0:T(8,128)(2,1)S(1)}, u32[]{:S(2)}, u32[]{:S(2)}) collective-permute-start(bf16[2,24,256]{2,1,0:T(8,128)(2,1)S(1)} %get-tuple-element.29), channel_id=1, source_target_pairs={{0,24},{4,28},{8,16},{12,20},{16,8},{20,12},{24,0},{28,4},{1,25},{... | collective-permute-start | bytes 73736 | tf_op jit(solution)/shard_map/ppermute | solution.py:40
  24.9 6.2 %collective-permute-start.11 = (bf16[32,256]{1,0:T(8,128)(2,1)S(1)}, bf16[32,256]{1,0:T(8,128)(2,1)S(1)}, u32[]{:S(2)}, u32[]{:S(2)}) collective-permute-start(bf16[32,256]{1,0:T(8,128)(2,1)S(1)} %get-tuple-element.35), channel_id=1, source_target_pairs={{0,8},{4,12},{8,0},{12,4},{16,24},{20,28},{24,16},{28,20},{1,9},{5... | collective-permute-start | bytes 49160 | tf_op jit(solution)/shard_map/ppermute | solution.py:40
  25.0 6.1 %collective-permute-start.12 = (bf16[32,256]{1,0:T(8,128)(2,1)S(1)}, bf16[32,256]{1,0:T(8,128)(2,1)S(1)}, u32[]{:S(2)}, u32[]{:S(2)}) collective-permute-start(bf16[32,256]{1,0:T(8,128)(2,1)S(1)} %get-tuple-element.36), channel_id=1, source_target_pairs={{0,16},{4,20},{8,24},{12,28},{16,0},{20,4},{24,8},{28,12},{1,17},{... | collective-permute-start | bytes 49160 | tf_op jit(solution)/shard_map/ppermute | solution.py:40
  25.9 5.5 %collective-permute-start.13 = (bf16[32,256]{1,0:T(8,128)(2,1)S(1)}, bf16[32,256]{1,0:T(8,128)(2,1)S(1)}, u32[]{:S(2)}, u32[]{:S(2)}) collective-permute-start(bf16[32,256]{1,0:T(8,128)(2,1)S(1)} %get-tuple-element.37), channel_id=1, source_target_pairs={{0,24},{4,28},{8,16},{12,20},{16,8},{20,12},{24,0},{28,4},{1,25},{... | collective-permute-start | bytes 49160 | tf_op jit(solution)/shard_map/ppermute | solution.py:40
